TPU v7x, 128 devices: a whole 4x4x4 slice. The times are simulated.
128 devices in a mesh: blk: 32 (over y_hi, x, z), head: 4 (over y_lo, core).
Axes of the slice: x: 4, y: 4 (y_hi: 2, y_lo: 2; y = y_hi * 2 + y_lo), z: 4, core: 2. Of those that a mesh axis runs over, the one named last changes fastest.
Arguments:
- states_in: bfloat16 [8192, 2048], P('blk'), may hold values from -12 to 12
- w_qkv: bfloat16 [3, 2048, 2048], P(None, None, 'head'), may hold values from -0.35355339 to 0.35355339
- qk_gain: float32 [2, 2048], P(None, 'head'), may hold values from 0.8 to 7.8
- w_out: bfloat16 [2048, 2048], P('head'), may hold values from -0.125 to 0.125
- post_gain: float32 [2, 2048], replicated, may hold values from 0.5 to 1.5
- w_gate_up: bfloat16 [2, 2048, 8192], P(None, None, 'blk'), may hold values from -0.125 to 0.125
- w_down: bfloat16 [8192, 2048], P('blk'), may hold values from -0.0625 to 0.0625
- cache_keys: bfloat16 [32, 256, 2048], P('blk', None, 'head'), may hold values from -6 to 6
- cache_values: bfloat16 [32, 256, 2048], P('blk', None, 'head'), may hold values from -6 to 6
- slot_node: int32 [32], replicated, may hold values from 0 to 31, each once
- node_length: int32 [32], replicated, may hold values from 1 to 256, 5120 in all
- node_parent: int32 [28], replicated, may hold values from 0 to 3
- leaf_segment: int32 [32, 256], replicated, may hold values from 0 to 7, never falling along the last dimension, each value on 1 to 128 neighbouring positions
- leaf_node: int32 [32, 8], replicated, may hold values from 4 to 31
Outputs:
- layer_out: bfloat16 [8192, 2048], P(('blk', 'head'))
Inputs may be any that keep to these rules, and one draw needn't show every extreme that they name: Slot s holds node slot_node[s]; every node is held once. Rows 0 to node_length[n] - 1 of node n's slot are valid; the longest node has 256 rows. Nodes 0 to 3 are roots; middle node 4 + i hangs under root node_parent[i]. `leaf_segment`: never falls along a group; every leaf of a group has 1 to 128 tokens. `leaf_node`: every leaf hangs under a middle node.
All inputs are finite; a program needn't handle non-finite values.
Results may differ from a plain program's by a relative error of at most 0.025.
Values may be sent and summed in bfloat16 or wider, within the bound.
No kernel may reach another device: no remote copies, remote signals or barrier semaphores. Data moves between devices by JAX's collectives and lax.ppermute only.
A program may use at most 192 MiB of HBM per device.

v0:
```python
import jax
import jax.numpy as jnp
from jax import lax
from jax.sharding import PartitionSpec as P

HD = 128
EPS = 1e-06
THETA = 500000.0
NEG = -1e30


def tree_info(leaf_segment, leaf_node, node_parent, node_length):
    groups, tok_rows = leaf_segment.shape
    leaf_count = leaf_node.shape[1]
    middles = node_parent.shape[0]
    all_nodes = node_length.shape[0]
    tenant_count = all_nodes - middles
    leaf_ids = jnp.arange(leaf_count, dtype=jnp.int32)
    onehot = (leaf_segment[:, :, None] == leaf_ids[None, None, :]).astype(jnp.int32)
    middle = jnp.sum(onehot * leaf_node[:, None, :], axis=-1)
    counts = jnp.sum(onehot, axis=1)
    starts = jnp.cumsum(counts, axis=1) - counts
    first_at = jnp.sum(onehot * starts[:, None, :], axis=-1)
    middle_ids = jnp.arange(middles, dtype=jnp.int32) + tenant_count
    root_node = jnp.sum(jnp.where(middle[..., None] == middle_ids, node_parent, 0), axis=-1)
    node_ids = jnp.arange(all_nodes, dtype=jnp.int32)
    len_middle = jnp.sum(jnp.where(middle[..., None] == node_ids, node_length, 0), axis=-1)
    len_root = jnp.sum(jnp.where(root_node[..., None] == node_ids, node_length, 0), axis=-1)
    offsets = jnp.arange(tok_rows, dtype=jnp.int32)[None, :] - first_at
    position = len_root + len_middle + offsets
    return (middle, root_node, position)


def rotate(values_in, position):
    half_size = values_in.shape[-1] // 2
    frequency = THETA ** (-2.0 * jnp.arange(half_size, dtype=jnp.float32) / values_in.shape[-1])
    angles = position.astype(jnp.float32)[:, None] * frequency[None, :]
    cosine = jnp.cos(angles)[:, None, :]
    sine_part = jnp.sin(angles)[:, None, :]
    lower = values_in[..., :half_size]
    upper = values_in[..., half_size:]
    return jnp.concatenate(
        [lower * cosine - upper * sine_part, upper * cosine + lower * sine_part], axis=-1
    )


def rms_norm(values_in, gain):
    return (
        values_in * lax.rsqrt(jnp.mean(values_in * values_in, axis=-1, keepdims=True) + EPS) * gain
    )


def lookup_length(nodes, node_length):
    node_ids = jnp.arange(node_length.shape[0], dtype=jnp.int32)
    return jnp.sum(jnp.where(nodes[:, None] == node_ids[None, :], node_length[None, :], 0), axis=-1)


def masked_partial(scores, visible, values_in):
    masked = jnp.where(visible, scores, NEG)
    peak = jnp.max(masked, axis=-1)
    weights = jnp.where(visible, jnp.exp(masked - peak[..., None]), 0.0)
    totals = jnp.sum(weights, axis=-1)
    summed = jnp.einsum(
        "rhk,khe->rhe", weights.astype(jnp.bfloat16), values_in, preferred_element_type=jnp.float32
    )
    return (peak, totals, summed)


def combine(left, right):
    peak = jnp.maximum(left[0], right[0])
    scale_left = jnp.exp(left[0] - peak)
    scale_right = jnp.exp(right[0] - peak)
    totals = left[1] * scale_left + right[1] * scale_right
    summed = left[2] * scale_left[..., None] + right[2] * scale_right[..., None]
    return (peak, totals, summed)


def cache_partial(queries, middle, root_node, keys_in, values_in, nodes, lengths):
    slots, node_rows, columns = keys_in.shape
    head_count, size = (queries.shape[1], queries.shape[2])
    flat_keys = keys_in.reshape(slots * node_rows, head_count, size)
    flat_values = values_in.reshape(slots * node_rows, head_count, size)
    node_flat = jnp.broadcast_to(nodes[:, None], (slots, node_rows)).reshape(-1)
    length_flat = jnp.broadcast_to(lengths[:, None], (slots, node_rows)).reshape(-1)
    row_flat = jnp.broadcast_to(
        jnp.arange(node_rows, dtype=jnp.int32)[None, :], (slots, node_rows)
    ).reshape(-1)
    visible = (
        (node_flat[None, :] == middle[:, None]) | (node_flat[None, :] == root_node[:, None])
    ) & (row_flat < length_flat)[None, :]
    scores = jnp.einsum(
        "rhe,khe->rhk", queries, flat_keys, preferred_element_type=jnp.float32
    ) * size ** (-0.5)
    return masked_partial(scores, visible[:, None, :], flat_values)


def on_device(
    states_in,
    w_qkv,
    qk_gain,
    w_out,
    post_gain,
    w_gate_up,
    w_down,
    cache_keys,
    cache_values,
    slot_node,
    node_length,
    node_parent,
    leaf_segment,
    leaf_node,
):
    blk_index = lax.axis_index("blk")
    head_index = lax.axis_index("head")
    head_devices = lax.axis_size("head")
    tok_rows = states_in.shape[0]
    heads_here = w_qkv.shape[2] // HD
    columns = w_qkv.shape[2] * head_devices
    qkv_raw = jnp.einsum("td,cdw->ctw", states_in, w_qkv, preferred_element_type=jnp.float32)
    query_squares, key_squares = lax.psum(
        (jnp.sum(qkv_raw[0] * qkv_raw[0], axis=1), jnp.sum(qkv_raw[1] * qkv_raw[1], axis=1)), "head"
    )
    middle_all, root_all, position_all = tree_info(
        leaf_segment, leaf_node, node_parent, node_length
    )
    position = lax.dynamic_index_in_dim(position_all, blk_index, 0, keepdims=False)
    middle_own = lax.dynamic_index_in_dim(middle_all, blk_index, 0, keepdims=False)
    root_own = lax.dynamic_index_in_dim(root_all, blk_index, 0, keepdims=False)
    segment_own = lax.dynamic_index_in_dim(leaf_segment, blk_index, 0, keepdims=False)

    def normed(raw_part, squares, gain):
        scaled = raw_part * lax.rsqrt(squares / columns + EPS)[:, None] * gain
        return rotate(scaled.reshape(tok_rows, heads_here, HD), position).astype(jnp.bfloat16)

    queries = normed(qkv_raw[0], query_squares, qk_gain[0])
    keys_new = normed(qkv_raw[1], key_squares, qk_gain[1])
    values_cast = qkv_raw[2].astype(jnp.bfloat16).reshape(tok_rows, heads_here, HD)
    order = jnp.arange(tok_rows, dtype=jnp.int32)
    see_leaf = (segment_own[:, None] == segment_own[None, :]) & (order[None, :] <= order[:, None])
    leaf_scores = jnp.einsum(
        "rhe,khe->rhk", queries, keys_new, preferred_element_type=jnp.float32
    ) * HD ** (-0.5)
    local_state = masked_partial(leaf_scores, see_leaf[:, None, :], values_cast)
    keys_piece = lax.all_gather(cache_keys, "blk", axis=0, tiled=True)
    values_piece = lax.all_gather(cache_values, "blk", axis=0, tiled=True)
    lengths = lookup_length(slot_node, node_length)
    needed = jnp.any(
        (slot_node[:, None] == middle_own[None, :]) | (slot_node[:, None] == root_own[None, :])
    )

    def attend(carry):
        return combine(
            carry,
            cache_partial(
                queries, middle_own, root_own, keys_piece, values_piece, slot_node, lengths
            ),
        )

    def keep(carry):
        return carry

    state = lax.cond(needed, attend, keep, local_state)
    attended = (
        (state[2] / state[1][..., None]).astype(jnp.bfloat16).reshape(tok_rows, heads_here * HD)
    )
    attn_part = jnp.dot(attended, w_out, preferred_element_type=jnp.float32)
    own_rows = tok_rows // head_devices
    attn_whole = lax.psum(attn_part.astype(jnp.bfloat16), "head").astype(jnp.float32)
    attn_proj = lax.dynamic_slice_in_dim(attn_whole, head_index * own_rows, own_rows, 0)
    state_rows = lax.dynamic_slice_in_dim(states_in, head_index * own_rows, own_rows, 0)
    mid_state = (state_rows.astype(jnp.float32) + rms_norm(attn_proj, post_gain[0])).astype(
        jnp.bfloat16
    )
    gate_up = jnp.einsum(
        "rd,cdf->crf",
        lax.all_gather(mid_state, "blk", axis=0, tiled=True),
        w_gate_up,
        preferred_element_type=jnp.float32,
    )
    hidden = (jax.nn.silu(gate_up[0]) * gate_up[1]).astype(jnp.bfloat16)
    mlp_proj = lax.psum_scatter(
        jnp.dot(hidden, w_down, preferred_element_type=jnp.float32).astype(jnp.bfloat16),
        "blk",
        scatter_dimension=0,
        tiled=True,
    ).astype(jnp.float32)
    return (mid_state.astype(jnp.float32) + rms_norm(mlp_proj, post_gain[1])).astype(jnp.bfloat16)


def solution(mesh):
    placed = (
        P("blk", None),
        P(None, None, "head"),
        P(None, "head"),
        P("head", None),
        P(),
        P(None, None, "blk"),
        P("blk", None),
        P("blk", None, "head"),
        P("blk", None, "head"),
        P(),
        P(),
        P(),
        P(),
        P(),
    )
    return jax.shard_map(
        on_device, mesh=mesh, in_specs=placed, out_specs=P(("blk", "head"), None), check_vma=False
    )
```

profile of v0, /device:TPU:0, one launch (start us, length us, event | category | flops | bytes accessed | tf_op | source)
XLA Modules:
  0.0 681.2 jit_solution(14530980794366099243)
XLA Ops:
  6.6 0.7 all-gather.4.cloned.1.call-update
  7.3 0.7 all-gather.6.cloned.1.call-update
  8.1 1.4 convert_reduce_fusion
  9.6 0.8 copy.50
  10.4 4.9 convolution_bitcast_fusion
  15.5 1.0 copy.53
  17.2 0.7 or_reduce_fusion
  18.5 7.1 %all-reduce = (f32[256]{0:T(256)S(1)}, f32[256]{0:T(256)S(1)}) all-reduce(f32[256]{0:T(256)S(1)} %get-tuple-element.109, f32[256]{0:T(256)S(1)} %get-tuple-element.108), channel_id=1, replica_groups=mesh['blk'=32,'head'=4] {'head'}, use_global_device_ids=true, to_apply=%region_11.12 | all-reduce | flops 512 | bytes 4096 | tf_op jit(solution)/shard_map/psum | solution.py:120
  25.6 0.6 select_reduce_fusion.2
  26.3 0.5 multiply_cosine_fusion
  26.9 1.1 multiply_multiply_fusion
  28.1 0.4 subtract_convert_fusion.1
  29.8 87.6 %all-gather.4.cloned.1.call-done = bf16[32,256,512]{2,1,0:T(8,128)(2,1)} async-done(((bf16[1,256,512]{2,1,0:T(8,128)(2,1)}), bf16[32,256,512]{2,1,0:T(8,128)(2,1)}) %all-gather.4.cloned.1.call-update) | async-done | bytes 8388624 | tf_op jit(solution)/shard_map/all_gather | solution.py:144
  117.3 105.1 %all-gather.6.cloned.1.call-done = bf16[32,256,512]{2,1,0:T(8,128)(2,1)} async-done(((bf16[1,256,512]{2,1,0:T(8,128)(2,1)}), bf16[32,256,512]{2,1,0:T(8,128)(2,1)}) %all-gather.6.cloned.1.call-update) | async-done | bytes 8388624 | tf_op jit(solution)/shard_map/all_gather | solution.py:145
  222.5 84.2 %conditional.1 = ((f32[256,4]{0,1:T(4,128)S(1)}, f32[256,4,128]{0,2,1:T(8,128)S(1)})) conditional(s32[]{:T(128)} %convert_element_type.61, (f32[256,4]{0,1:T(4,128)S(1)}, f32[256,4,128]{0,2,1:T(8,128)S(1)}) %tuple.12, (s32[32]{0:T(128)S(1)}, s32[256]{0:T(256)S(1)}, s32[256]{0:T(256)S(1)}, s32[32,32]{1,0:T(8,128)S(1)}, s32[32]{0:T(128)S(1)}, ...), branch_computations={%region_14.15_spmd, %region_15.19_spmd} | conditional | flops 4412816384 | bytes 163015328 | solution.py:162
  222.9 6.9 %or_and_fusion = pred[256,8192]{0,1:T(8,128)(4,1)} fusion(s32[256]{0:T(256)S(1)} %get-tuple-element.44, s32[256]{0:T(256)S(1)} %get-tuple-element.43, s32[8192]{0:T(1024)S(1)} %bitcast.80, pred[8192]{0:T(1024)(128)(4,1)S(1)} %lt.18), kind=kLoop, calls=%fused_computation.10 | loop fusion | flops 8388608 | bytes 2140160 | tf_op jit(solution)/shard_map/cond/branch_1_fun/and | solution.py:88
  229.7 12.5 %reshape.255 = bf16[8192,4,128]{2,1,0:T(4,128)(2,1)} reshape(bf16[32,256,512]{2,1,0:T(8,128)(2,1)} %get-tuple-element.47) | data formatting | bytes 16777216 | tf_op jit(solution)/shard_map/cond/branch_1_fun/reshape | solution.py:81
  242.2 16.4 %fusion = (f32[256,4]{0,1:T(4,128)S(1)}, f32[4,8192,256]{2,1,0:T(8,128)}) fusion(pred[256,8192]{0,1:T(8,128)(4,1)} %or_and_fusion, bf16[256,4,128]{2,0,1:T(8,128)(2,1)S(1)} %get-tuple-element.48, bf16[8192,4,128]{2,1,0:T(4,128)(2,1)} %reshape.255), kind=kOutput, calls=%fused_computation.2 | convolution fusion | flops 2172648448 | bytes 44306432 | tf_op jit(solution)/shard_map/cond/branch_1_fun/rhe,khe->rhk/dot_general | solution.py:91
  258.6 15.1 %fusion.2 = f32[256,4]{0,1:T(4,128)S(1)} fusion(f32[4,8192,256]{2,1,0:T(8,128)} %get-tuple-element.120, f32[256,4]{0,1:T(4,128)S(1)} %get-tuple-element.119, pred[256,8192]{0,1:T(8,128)(4,1)} %or_and_fusion), kind=kLoop, calls=%fused_computation.4 | loop fusion | flops 41942016 | bytes 35659776 | tf_op jit(solution)/shard_map/cond/branch_1_fun/reduce_sum | solution.py:62
  273.8 12.5 %reshape.256 = bf16[8192,4,128]{2,1,0:T(4,128)(2,1)} reshape(bf16[32,256,512]{2,1,0:T(8,128)(2,1)} %get-tuple-element.50) | data formatting | bytes 16777216 | tf_op jit(solution)/shard_map/cond/branch_1_fun/reshape | solution.py:82
  286.3 1.0 copy.56
  287.3 19.1 %fusion.19 = f32[256,4,128]{2,0,1:T(8,128)S(1)} fusion(bf16[8192,4,128]{2,1,0:T(4,128)(2,1)} %reshape.256, f32[4,8192,256]{2,1,0:T(8,128)} %get-tuple-element.120, f32[256,4]{0,1:T(4,128)S(1)} %get-tuple-element.119, pred[256,8192]{0,1:T(8,128)(4,1)} %or_and_fusion, f32[256,4,128]{2,0,1:T(8,128)} %copy.56, f32[256,4]{0,1:T(4,128)S(1)} %get-tuple-element.118, ...), kind=kOutput, calls=%fused_computation.13 | convolution fusion | flops 2189819904 | bytes 45101056 | tf_op jit(solution)/shard_map/cond/branch_1_fun/rhk,khe->rhe/dot_general | solution.py:63
  306.7 3.4 convolution_convert_fusion.1
  310.2 39.3 %all-reduce.3.cloned.1.call-done = bf16[256,2048]{1,0:T(8,128)(2,1)} async-done(((bf16[256,2048]{1,0:T(8,128)(2,1)}), bf16[256,2048]{1,0:T(8,128)(2,1)}) %all-reduce.3.cloned.1.call-update) | async-done | bytes 1048592 | tf_op jit(solution)/shard_map/psum | solution.py:168
  349.5 1.1 fusion.46
  350.6 1.9 fusion.45
  352.8 105.4 %all-gather.8.cloned.1.call-done = bf16[2048,2048]{1,0:T(8,128)(2,1)} async-done(((bf16[64,2048]{1,0:T(8,128)(2,1)}), bf16[2048,2048]{1,0:T(8,128)(2,1)}) %all-gather.8.cloned.1.call-update) | async-done | bytes 8388624 | tf_op jit(solution)/shard_map/all_gather | solution.py:176
  458.2 6.9 %fusion.31 = f32[2,2048,256]{2,1,0:T(8,128)S(1)} fusion(bf16[2,2048,256]{2,1,0:T(8,128)(2,1)S(1)} %copy-done, bf16[2048,2048]{1,0:T(8,128)(2,1)} %all-gather.8.cloned.1.call-done), kind=kOutput, calls=%fused_computation.28 | convolution fusion | flops 4294967296 | bytes 14680064 | tf_op jit(solution)/shard_map/rd,cdf->crf/dot_general | solution.py:174
  465.1 5.7 convolution_convert_fusion
  470.8 201.0 %reduce-scatter.2.cloned.1.call-done = bf16[64,2048]{1,0:T(8,128)(2,1)} async-done(((bf16[2048,2048]{1,0:T(8,128)(2,1)}), bf16[64,2048]{1,0:T(8,128)(2,1)}) %reduce-scatter.2.cloned.1.call-update) | async-done | bytes 262160 | tf_op jit(solution)/shard_map/reduce_scatter | solution.py:181
  671.7 1.1 fusion.47
  672.9 1.8 fusion.50
  (57 shorter events, 3.4 us)
Async XLA Ops:
  6.5 451.7 %copy-start = (bf16[2,2048,256]{2,1,0:T(8,128)(2,1)S(1)}, bf16[2,2048,256]{2,1,0:T(8,128)(2,1)}, u32[]{:S(2)}) copy-start(bf16[2,2048,256]{2,1,0:T(8,128)(2,1)} %param.21) | copy-start | bytes 6291460
  6.5 10.2 %copy-start.2 = (s32[32,256]{1,0:T(8,128)S(1)}, s32[32,256]{1,0:T(8,128)}, u32[]{:S(2)}) copy-start(s32[32,256]{1,0:T(8,128)} %param.28) | copy-start | bytes 98308
  6.5 10.4 %copy-start.7 = (s32[28]{0:T(128)S(1)}, s32[28]{0:T(128)}, u32[]{:S(2)}) copy-start(s32[28]{0:T(128)} %param.27) | copy-start | bytes 340
  6.5 10.6 %copy-start.4 = (s32[32]{0:T(128)S(1)}, s32[32]{0:T(128)}, u32[]{:S(2)}) copy-start(s32[32]{0:T(128)} %param.25) | copy-start | bytes 388
  6.5 19.1 %copy-start.6 = (s32[32]{0:T(128)S(1)}, s32[32]{0:T(128)}, u32[]{:S(2)}) copy-start(s32[32]{0:T(128)} %param.26) | copy-start | bytes 388
  6.5 110.8 %all-gather.4.cloned.1.call-start = ((), (), s32[]{:S(2)}) async-start(), calls=%async_computation.1 | async-start | bytes 8650752 | tf_op jit(solution)/shard_map/all_gather | solution.py:144
  7.3 19.0 %copy-start.5 = (f32[2,512]{1,0:T(2,128)S(1)}, f32[2,512]{1,0:T(2,128)}, u32[]{:S(2)}) copy-start(f32[2,512]{1,0:T(2,128)} %param.18) | copy-start | bytes 12292
  7.3 215.2 %all-gather.6.cloned.1.call-start = ((), (), s32[]{:S(2)}) async-start(), calls=%async_computation.2 | async-start | bytes 8650752 | tf_op jit(solution)/shard_map/all_gather | solution.py:145
  8.0 341.4 %all-reduce.3.cloned.1.call-start = ((), (), s32[]{:S(2)}) async-start(), calls=%async_computation.3 | async-start | bytes 2097152 | tf_op jit(solution)/shard_map/psum | solution.py:168
  222.5 87.7 %copy-start.3 = (f32[2,2048]{1,0:T(2,128)S(1)}, f32[2,2048]{1,0:T(2,128)}, u32[]{:S(2)}) copy-start(f32[2,2048]{1,0:T(2,128)} %param.20) | copy-start | bytes 49156
  310.1 148.1 %all-gather.8.cloned.1.call-start = ((), (), s32[]{:S(2)}) async-start(), calls=%async_computation.4 | async-start | bytes 8650752 | tf_op jit(solution)/shard_map/all_gather | solution.py:176
  352.5 112.5 %copy-start.8 = (bf16[256,2048]{1,0:T(8,128)(2,1)S(1)}, bf16[256,2048]{1,0:T(8,128)(2,1)}, u32[]{:S(2)}) copy-start(bf16[256,2048]{1,0:T(8,128)(2,1)} %param.22) | copy-start | bytes 3145732
  352.5 319.2 %reduce-scatter.2.cloned.1.call-start = ((), (), s32[]{:S(2)}) async-start(), calls=%async_computation.5 | async-start | bytes 8650752 | tf_op jit(solution)/shard_map/reduce_scatter | solution.py:181
  470.7 202.1 %copy-start.1 = (bf16[64,2048]{1,0:T(8,128)(2,1)S(1)}, bf16[64,2048]{1,0:T(8,128)(2,1)}, u32[]{:S(2)}) copy-start(bf16[64,2048]{1,0:T(8,128)(2,1)} %fusion.45) | copy-start | bytes 786436
Sparse Core Ops, SparseCore 0:
  10.5 106.7 all-gather.3
  120.4 101.9 all-gather.5
  310.2 39.2 all-reduce.2
  352.9 105.2 all-gather.7
  470.9 200.8 reduce-scatter.1
where the time goes:
time: 682 us; the launch traced here: 681 us
  waiting for transfers between devices  540 us (79%)
  matrix products  57 us (8%)
  other arithmetic  34.4 us (5%)
  local copies, waits for them, and re-layouts  28.5 us (4%)
  between operations  14.1 us (2%)
  blocking collectives  7.07 us (1%)
    reduce_scatter x1, waiting for transfers between devices, on_device(): lax.psum_scatter(jnp.dot(hidden, w_down, preferred_element_type=jnp.float...  201 us
    all_gather x1, waiting for transfers between devices, on_device(): lax.all_gather(mid_state, 'blk', axis=0, tiled=True)  105 us
    all_gather x1, waiting for transfers between devices, on_device(): values_piece = lax.all_gather(cache_values, 'blk', axis=0, tiled=True)  105 us
    all_gather x1, waiting for transfers between devices, on_device(): keys_piece = lax.all_gather(cache_keys, 'blk', axis=0, tiled=True)  87.6 us
    psum x1, waiting for transfers between devices, on_device(): lax.psum(attn_part.astype(jnp.bfloat16), 'head').astype(jnp.float32)  39.3 us
    dot_general x2, matrix products, masked_partial(): jnp.einsum('rhk,khe->rhe', weights.astype(jnp.bfloat16), values_in, prefe...  19.5 us
    dot_general x1, matrix products, cache_partial(): jnp.einsum('rhe,khe->rhk', queries, flat_keys, preferred_element_type=jnp...  16.4 us
    reduce_sum x2, other arithmetic, masked_partial(): totals = jnp.sum(weights, axis=-1)  15.3 us
  transfers between devices with their start and end apart: 5, of which 5 were waited for; matrix products, arithmetic and copies ran while one was open for 2% of the time, Pallas kernels for 0%

commit v1 on v0

--- a/solution.py
+++ b/solution.py
@@ -173,7 +173,9 @@
     )
     gate_up = jnp.einsum(
         "rd,cdf->crf",
-        lax.all_gather(mid_state, "blk", axis=0, tiled=True),
+        jnp.concatenate(
+            lax.all_to_all(jnp.stack([mid_state] * lax.axis_size("blk")), "blk", 0, 0), axis=0
+        ),
         w_gate_up,
         preferred_element_type=jnp.float32,
     )

time: 682 us -> 687 us (level)
  blocking collectives: 7.07 us -> 115 us
  waiting for transfers between devices: 540 us -> 439 us
    all_to_all x0 -> x1, blocking collectives: none -> 108 us  [on_device(): lax.all_to_all(jnp.stack([mid_state] * lax.axis_size('blk')), 'blk', 0, 0)]
    all_gather x1 -> x0, waiting for transfers between devices: 105 us -> none  [on_device(): lax.all_gather(mid_state, 'blk', axis=0, tiled=True)]
  transfers between devices with their start and end apart: 5 -> 4, of which waited for: 5 -> 4; matrix products, arithmetic and copies ran while one was open for 2% -> 2% of each run, Pallas kernels for 0% -> 0%
where the time goes in v1:
time: 687 us; the launch traced here: 685 us
  waiting for transfers between devices  439 us (64%)
  blocking collectives  115 us (17%)
  matrix products  54.7 us (8%)
  other arithmetic  33.7 us (5%)
  local copies, waits for them, and re-layouts  29.5 us (4%)
  between operations  14 us (2%)
    reduce_scatter x1, waiting for transfers between devices, on_device(): lax.psum_scatter(jnp.dot(hidden, w_down, preferred_element_type=jnp.float...  205 us
    all_to_all x1, blocking collectives, on_device(): lax.all_to_all(jnp.stack([mid_state] * lax.axis_size('blk')), 'blk', 0, 0)  108 us
    all_gather x1, waiting for transfers between devices, on_device(): values_piece = lax.all_gather(cache_values, 'blk', axis=0, tiled=True)  105 us
    all_gather x1, waiting for transfers between devices, on_device(): keys_piece = lax.all_gather(cache_keys, 'blk', axis=0, tiled=True)  87.6 us
    psum x1, waiting for transfers between devices, on_device(): lax.psum(attn_part.astype(jnp.bfloat16), 'head').astype(jnp.float32)  39.3 us
    dot_general x2, matrix products, masked_partial(): jnp.einsum('rhk,khe->rhe', weights.astype(jnp.bfloat16), values_in, prefe...  19.5 us
    dot_general x1, matrix products, cache_partial(): jnp.einsum('rhe,khe->rhk', queries, flat_keys, preferred_element_type=jnp...  16.4 us
    reduce_sum x2, other arithmetic, masked_partial(): totals = jnp.sum(weights, axis=-1)  15.3 us
  transfers between devices with their start and end apart: 4, of which 4 were waited for; matrix products, arithmetic and copies ran while one was open for 2% of the time, Pallas kernels for 0%

profile of v1, /device:TPU:0, one launch (start us, length us, event | category | flops | bytes accessed | tf_op | source)
XLA Modules:
  0.0 685.5 jit_solution(989611545305038534)
XLA Ops:
  6.6 0.7 all-gather.3.cloned.1.call-update
  7.3 0.7 all-gather.5.cloned.1.call-update
  8.1 1.4 convert_reduce_fusion
  9.6 0.8 copy.50
  10.4 4.9 convolution_bitcast_fusion.1
  15.5 1.0 copy.53
  17.2 0.7 or_reduce_fusion
  18.5 7.1 %all-reduce = (f32[256]{0:T(256)S(1)}, f32[256]{0:T(256)S(1)}) all-reduce(f32[256]{0:T(256)S(1)} %get-tuple-element.109, f32[256]{0:T(256)S(1)} %get-tuple-element.108), channel_id=1, replica_groups=mesh['blk'=32,'head'=4] {'head'}, use_global_device_ids=true, to_apply=%region_11.12 | all-reduce | flops 512 | bytes 4096 | tf_op jit(solution)/shard_map/psum | solution.py:120
  25.6 0.6 select_reduce_fusion.2
  26.3 0.5 multiply_cosine_fusion
  26.9 1.1 multiply_multiply_fusion
  29.8 87.6 %all-gather.3.cloned.1.call-done = bf16[32,256,512]{2,1,0:T(8,128)(2,1)} async-done(((bf16[1,256,512]{2,1,0:T(8,128)(2,1)}), bf16[32,256,512]{2,1,0:T(8,128)(2,1)}) %all-gather.3.cloned.1.call-update) | async-done | bytes 8388624 | tf_op jit(solution)/shard_map/all_gather | solution.py:144
  117.3 105.1 %all-gather.5.cloned.1.call-done = bf16[32,256,512]{2,1,0:T(8,128)(2,1)} async-done(((bf16[1,256,512]{2,1,0:T(8,128)(2,1)}), bf16[32,256,512]{2,1,0:T(8,128)(2,1)}) %all-gather.5.cloned.1.call-update) | async-done | bytes 8388624 | tf_op jit(solution)/shard_map/all_gather | solution.py:145
  222.5 84.2 %conditional.1 = ((f32[256,4]{0,1:T(4,128)S(1)}, f32[256,4,128]{0,2,1:T(8,128)S(1)})) conditional(s32[]{:T(128)} %convert_element_type.61, (f32[256,4]{0,1:T(4,128)S(1)}, f32[256,4,128]{0,2,1:T(8,128)S(1)}) %tuple.12, (s32[32]{0:T(128)S(1)}, s32[256]{0:T(256)S(1)}, s32[256]{0:T(256)S(1)}, s32[32,32]{1,0:T(8,128)S(1)}, s32[32]{0:T(128)S(1)}, ...), branch_computations={%region_14.15_spmd, %region_15.19_spmd} | conditional | flops 4412816384 | bytes 163015328 | solution.py:162
  222.9 6.9 %or_and_fusion = pred[256,8192]{0,1:T(8,128)(4,1)} fusion(s32[256]{0:T(256)S(1)} %get-tuple-element.44, s32[256]{0:T(256)S(1)} %get-tuple-element.43, s32[8192]{0:T(1024)S(1)} %bitcast.80, pred[8192]{0:T(1024)(128)(4,1)S(1)} %lt.18), kind=kLoop, calls=%fused_computation.10 | loop fusion | flops 8388608 | bytes 2140160 | tf_op jit(solution)/shard_map/cond/branch_1_fun/and | solution.py:88
  229.7 12.5 %reshape.259 = bf16[8192,4,128]{2,1,0:T(4,128)(2,1)} reshape(bf16[32,256,512]{2,1,0:T(8,128)(2,1)} %get-tuple-element.47) | data formatting | bytes 16777216 | tf_op jit(solution)/shard_map/cond/branch_1_fun/reshape | solution.py:81
  242.2 16.4 %fusion = (f32[256,4]{0,1:T(4,128)S(1)}, f32[4,8192,256]{2,1,0:T(8,128)}) fusion(pred[256,8192]{0,1:T(8,128)(4,1)} %or_and_fusion, bf16[256,4,128]{2,0,1:T(8,128)(2,1)S(1)} %get-tuple-element.48, bf16[8192,4,128]{2,1,0:T(4,128)(2,1)} %reshape.259), kind=kOutput, calls=%fused_computation.2 | convolution fusion | flops 2172648448 | bytes 44306432 | tf_op jit(solution)/shard_map/cond/branch_1_fun/rhe,khe->rhk/dot_general | solution.py:91
  258.6 15.1 %fusion.2 = f32[256,4]{0,1:T(4,128)S(1)} fusion(f32[4,8192,256]{2,1,0:T(8,128)} %get-tuple-element.120, f32[256,4]{0,1:T(4,128)S(1)} %get-tuple-element.119, pred[256,8192]{0,1:T(8,128)(4,1)} %or_and_fusion), kind=kLoop, calls=%fused_computation.4 | loop fusion | flops 41942016 | bytes 35659776 | tf_op jit(solution)/shard_map/cond/branch_1_fun/reduce_sum | solution.py:62
  273.8 12.5 %reshape.260 = bf16[8192,4,128]{2,1,0:T(4,128)(2,1)} reshape(bf16[32,256,512]{2,1,0:T(8,128)(2,1)} %get-tuple-element.50) | data formatting | bytes 16777216 | tf_op jit(solution)/shard_map/cond/branch_1_fun/reshape | solution.py:82
  286.3 1.0 copy.56
  287.3 19.1 %fusion.19 = f32[256,4,128]{2,0,1:T(8,128)S(1)} fusion(bf16[8192,4,128]{2,1,0:T(4,128)(2,1)} %reshape.260, f32[4,8192,256]{2,1,0:T(8,128)} %get-tuple-element.120, f32[256,4]{0,1:T(4,128)S(1)} %get-tuple-element.119, pred[256,8192]{0,1:T(8,128)(4,1)} %or_and_fusion, f32[256,4,128]{2,0,1:T(8,128)} %copy.56, f32[256,4]{0,1:T(4,128)S(1)} %get-tuple-element.118, ...), kind=kOutput, calls=%fused_computation.13 | convolution fusion | flops 2189819904 | bytes 45101056 | tf_op jit(solution)/shard_map/cond/branch_1_fun/rhk,khe->rhe/dot_general | solution.py:63
  306.7 3.4 convolution_convert_fusion.1
  310.2 39.3 %all-reduce.3.cloned.1.call-done = bf16[256,2048]{1,0:T(8,128)(2,1)} async-done(((bf16[256,2048]{1,0:T(8,128)(2,1)}), bf16[256,2048]{1,0:T(8,128)(2,1)}) %all-reduce.3.cloned.1.call-update) | async-done | bytes 1048592 | tf_op jit(solution)/shard_map/psum | solution.py:168
  349.5 1.1 fusion.41
  350.6 1.2 fusion.40
  351.8 1.1 stack.2
  352.9 107.6 %all_to_all.5 = bf16[32,64,2048]{2,1,0:T(8,128)(2,1)S(1)} all-to-all(bf16[32,64,2048]{2,1,0:T(8,128)(2,1)S(1)} %stack.2), channel_id=1, replica_groups=mesh['blk'=32,'head'=4] {'blk'}, dimensions={0} | all-to-all | bytes 16777216 | tf_op jit(solution)/shard_map/all_to_all | solution.py:177
  460.5 4.5 convolution_bitcast_fusion
  465.0 5.6 convolution_convert_fusion
  470.7 205.3 %reduce-scatter.2.cloned.1.call-done = bf16[64,2048]{1,0:T(8,128)(2,1)} async-done(((bf16[2048,2048]{1,0:T(8,128)(2,1)}), bf16[64,2048]{1,0:T(8,128)(2,1)}) %reduce-scatter.2.cloned.1.call-update) | async-done | bytes 262160 | tf_op jit(solution)/shard_map/reduce_scatter | solution.py:183
  676.0 1.1 fusion.42
  677.1 1.8 fusion.45
  (54 shorter events, 3.6 us)
Async XLA Ops:
  6.5 454.0 %copy-start = (bf16[2,2048,256]{2,1,0:T(8,128)(2,1)S(1)}, bf16[2,2048,256]{2,1,0:T(8,128)(2,1)}, u32[]{:S(2)}) copy-start(bf16[2,2048,256]{2,1,0:T(8,128)(2,1)} %param.21) | copy-start | bytes 6291460
  6.5 10.2 %copy-start.1 = (s32[32,256]{1,0:T(8,128)S(1)}, s32[32,256]{1,0:T(8,128)}, u32[]{:S(2)}) copy-start(s32[32,256]{1,0:T(8,128)} %param.28) | copy-start | bytes 98308
  6.5 10.4 %copy-start.6 = (s32[28]{0:T(128)S(1)}, s32[28]{0:T(128)}, u32[]{:S(2)}) copy-start(s32[28]{0:T(128)} %param.27) | copy-start | bytes 340
  6.5 10.6 %copy-start.3 = (s32[32]{0:T(128)S(1)}, s32[32]{0:T(128)}, u32[]{:S(2)}) copy-start(s32[32]{0:T(128)} %param.25) | copy-start | bytes 388
  6.5 19.1 %copy-start.5 = (s32[32]{0:T(128)S(1)}, s32[32]{0:T(128)}, u32[]{:S(2)}) copy-start(s32[32]{0:T(128)} %param.26) | copy-start | bytes 388
  6.5 110.8 %all-gather.3.cloned.1.call-start = ((), (), s32[]{:S(2)}) async-start(), calls=%async_computation.2 | async-start | bytes 8650752 | tf_op jit(solution)/shard_map/all_gather | solution.py:144
  7.3 19.0 %copy-start.4 = (f32[2,512]{1,0:T(2,128)S(1)}, f32[2,512]{1,0:T(2,128)}, u32[]{:S(2)}) copy-start(f32[2,512]{1,0:T(2,128)} %param.18) | copy-start | bytes 12292
  7.3 215.2 %all-gather.5.cloned.1.call-start = ((), (), s32[]{:S(2)}) async-start(), calls=%async_computation.3 | async-start | bytes 8650752 | tf_op jit(solution)/shard_map/all_gather | solution.py:145
  8.0 341.4 %all-reduce.3.cloned.1.call-start = ((), (), s32[]{:S(2)}) async-start(), calls=%async_computation.4 | async-start | bytes 2097152 | tf_op jit(solution)/shard_map/psum | solution.py:168
  222.5 87.7 %copy-start.2 = (f32[2,2048]{1,0:T(2,128)S(1)}, f32[2,2048]{1,0:T(2,128)}, u32[]{:S(2)}) copy-start(f32[2,2048]{1,0:T(2,128)} %param.20) | copy-start | bytes 49156
  310.1 365.9 %reduce-scatter.2.cloned.1.call-start = ((), (), s32[]{:S(2)}) async-start(), calls=%async_computation.5 | async-start | bytes 8650752 | tf_op jit(solution)/shard_map/reduce_scatter | solution.py:183
  460.5 4.5 copy-start.7
Sparse Core Ops, SparseCore 0:
  10.5 106.7 all-gather.2
  120.4 101.9 all-gather.4
  310.2 39.2 all-reduce.2
  470.8 205.1 reduce-scatter.1
